TPU v7x, 256 devices: a whole 4x4x8 slice. The times are simulated.
256 devices in a mesh: dp: 16 (over x, y), expert: 16 (over z, core).
Axes of the slice: x: 4, y: 4, z: 8, core: 2. Of those that a mesh axis runs over, the one named last changes fastest.
Arguments:
- tokens: bfloat16 [32768, 2048], P(('dp', 'expert')), may hold values from -24 to 24
- routes: int32 [32768, 2], P(('dp', 'expert')), may hold values from 0 to 7, all different within a row; in each aligned block of 128 rows (0 to 127, 128 to 255, ...) at most 36 rows name the same one
- gates: int32 [32768, 2], P(('dp', 'expert')), may hold values from 1 to 1023
- cotangent: bfloat16 [32768, 2048], P(('dp', 'expert')), may hold values from -6 to 6
- w_gate: bfloat16 [2048, 8192], P(None, 'expert'), may hold values from -0.125 to 0.125
- w_up: bfloat16 [2048, 8192], P(None, 'expert'), may hold values from -0.125 to 0.125
- w_down: bfloat16 [8192, 2048], P('expert'), may hold values from -0.1875 to 0.1875
Outputs:
- mixed: bfloat16 [32768, 2048], P(('dp', 'expert'))
- input_grad: bfloat16 [32768, 2048], P(('dp', 'expert'))
- grad_gate: float32 [2048, 8192], P('dp', 'expert')
- grad_up: float32 [2048, 8192], P('dp', 'expert')
- grad_down: float32 [8192, 2048], P('expert', 'dp')
Inputs may be any that keep to these rules, and one draw needn't show every extreme that they name: `routes`: the two experts of a token differ. In the rows of one device no expert is named by more than 36 pairs, a bound that some block reaches.
All inputs are finite; a program needn't handle non-finite values.
Results may differ from a plain program's by a relative error of at most 0.0064.
Values may be sent and summed in bfloat16 or wider, within the bound.
A program may use at most 128 MiB of HBM per device.

v0:
```python
import jax
import jax.numpy as jnp
from jax import lax
from jax.sharding import PartitionSpec as P

EXPERTS = 8
CAP = 36


def slot_table(pairs):
    count = pairs.shape[0]
    onehot = (pairs[:, None] == jnp.arange(EXPERTS, dtype=jnp.int32)[None, :]).astype(jnp.int32)
    before = jnp.cumsum(onehot, axis=0) - onehot
    position = jnp.sum(before * onehot, axis=1)
    table = jnp.full((EXPERTS * CAP,), count, jnp.int32)
    table = table.at[pairs * CAP + position].set(jnp.arange(count, dtype=jnp.int32))
    return (position, table)


def contract_rows(left, right):
    return lax.dot_general(
        left, right, (((0,), (0,)), ((), ())), preferred_element_type=jnp.float32
    )


def contract_cols(left, right):
    return lax.dot_general(
        left, right, (((1,), (1,)), ((), ())), preferred_element_type=jnp.float32
    )


def per_device(tokens, routes, gates, cotangent, w_gate, w_up, w_down):
    tok_dev, width = tokens.shape
    devices = lax.axis_size("expert")
    tiles = devices // EXPERTS
    slots = devices * CAP
    hidden = w_gate.shape[1]
    pairs = routes.reshape(-1)
    position, table = slot_table(pairs)
    send_index = jnp.broadcast_to(table.reshape(EXPERTS, 1, CAP), (EXPERTS, tiles, CAP)).reshape(-1)
    zero_row = jnp.zeros((1, width), jnp.bfloat16)
    factor = gates.reshape(-1).astype(jnp.float32) / 1024.0
    factor_pad = jnp.concatenate([factor, jnp.zeros((1,), jnp.float32)])
    padded_x = jnp.concatenate([tokens, zero_row])
    padded_dy = jnp.concatenate([cotangent, zero_row])
    x_send = jnp.take(padded_x, send_index // 2, axis=0).reshape(devices, CAP, width)
    slot_factor = jnp.take(factor_pad, send_index, axis=0)
    dy_rows = jnp.take(padded_dy, send_index // 2, axis=0)
    dz_send = (
        (slot_factor[:, None] * dy_rows.astype(jnp.float32))
        .astype(jnp.bfloat16)
        .reshape(devices, CAP, width)
    )
    w_both = jnp.concatenate([w_gate, w_up], axis=1)
    x_recv = lax.all_to_all(x_send, "expert", split_axis=0, concat_axis=0, tiled=True)
    forward_xrows = x_recv.reshape(slots, width)
    joined = jnp.dot(forward_xrows, w_both, preferred_element_type=jnp.float32)
    a = joined[:, :hidden]
    b = joined[:, hidden:]
    sig = jax.nn.sigmoid(a)
    act = a * sig
    forward_h = (act * b).astype(jnp.bfloat16)
    z = jnp.dot(forward_h, w_down, preferred_element_type=jnp.float32).astype(jnp.bfloat16)
    xrows, a, b, sig, act, h, z = (
        forward_xrows,
        a,
        b,
        sig,
        act,
        forward_h,
        z.reshape(devices, CAP, width),
    )
    z_back = lax.all_to_all(z, "expert", split_axis=0, concat_axis=0, tiled=True)
    dz_recv = lax.all_to_all(dz_send, "expert", split_axis=0, concat_axis=0, tiled=True)
    backward_dz = dz_recv.reshape(slots, width)
    dh = contract_cols(backward_dz, w_down)
    dsilu = sig * (1.0 + a * (1.0 - sig))
    d_gate = (dh * b * dsilu).astype(jnp.bfloat16)
    d_up = (dh * act).astype(jnp.bfloat16)
    backward_both_grads = jnp.concatenate([d_gate, d_up], axis=1)
    dx = contract_cols(backward_both_grads, w_both).astype(jnp.bfloat16)
    dz, both_grads, dx = (backward_dz, backward_both_grads, dx.reshape(devices, CAP, width))
    dx_back = lax.all_to_all(dx, "expert", split_axis=0, concat_axis=0, tiled=True)
    pair_slot = pairs * CAP + position

    def combine(back):
        summed = jnp.sum(back.reshape(EXPERTS, tiles, CAP, width).astype(jnp.float32), axis=1)
        return jnp.take(summed.reshape(EXPERTS * CAP, width), pair_slot, axis=0)

    mixed = jnp.sum((factor[:, None] * combine(z_back)).reshape(tok_dev, 2, width), axis=1).astype(
        jnp.bfloat16
    )
    input_grad = jnp.sum(combine(dx_back).reshape(tok_dev, 2, width), axis=1).astype(jnp.bfloat16)
    summed = lax.psum_scatter(
        jnp.concatenate([contract_rows(xrows, both_grads), contract_rows(dz, h)], axis=1),
        "dp",
        scatter_dimension=0,
        tiled=True,
    )
    grad_gate = summed[:, :hidden]
    grad_up = summed[:, hidden : 2 * hidden]
    grad_down = summed[:, 2 * hidden :].T
    return (mixed, input_grad, grad_gate, grad_up, grad_down)


def solution(mesh):
    in_specs = (
        P(("dp", "expert"), None),
        P(("dp", "expert"), None),
        P(("dp", "expert"), None),
        P(("dp", "expert"), None),
        P(None, "expert"),
        P(None, "expert"),
        P("expert", None),
    )
    out_specs = (
        P(("dp", "expert"), None),
        P(("dp", "expert"), None),
        P("dp", "expert"),
        P("dp", "expert"),
        P("expert", "dp"),
    )
    return jax.shard_map(
        per_device, mesh=mesh, in_specs=in_specs, out_specs=out_specs, check_vma=False
    )
```

profile of v0, /device:TPU:1, one launch (start us, length us, event | category | flops | bytes accessed | tf_op | source)
XLA Modules:
  0.0 371.6 jit_solution(4687582518789328863)
XLA Ops:
  7.2 0.8 broadcast_multiply_fusion
  8.0 0.8 copy.15
  9.3 0.6 reduce-window.6
  10.3 1.4 scatter_custom_fusion
  12.1 1.1 concatenate.18
  13.1 4.0 %gather_fusion.1 = bf16[576,2048]{1,0:T(8,128)(2,1)} fusion(bf16[129,2048]{1,0:T(8,128)(2,1)S(1)} %concatenate.18, s32[1024]{0:T(1024)S(1)} %get-tuple-element.30), kind=kCustom, calls=%fused_computation.clone | custom fusion | bytes 4720896 | tf_op jit(solution)/shard_map/jit(_take)/gather | solution.py:46
  17.2 3.4 broadcast_select_fusion
  20.5 4.1 %reshape.168 = bf16[16,36,2048]{2,1,0:T(8,128)(2,1)} reshape(bf16[576,2048]{1,0:T(8,128)(2,1)} %broadcast_select_fusion) | data formatting | bytes 4718592 | tf_op jit(solution)/shard_map/reshape | solution.py:46
  24.6 10.1 %all-to-all-start = ((bf16[16,36,2048]{2,1,0:T(8,128)(2,1)}), bf16[16,36,2048]{2,1,0:T(8,128)(2,1)}, u32[]{:S(2)}, u32[]{:S(2)}) async-start(bf16[16,36,2048]{2,1,0:T(8,128)(2,1)} %reshape.168), calls=%async_computation | async-start | bytes 5242880 | tf_op jit(solution)/shard_map/all_to_all | solution.py:55
  35.0 4.1 %gather_fusion.3 = bf16[576,2048]{1,0:T(8,128)(2,1)} fusion(bf16[129,2048]{1,0:T(8,128)(2,1)S(1)} %concatenate.21, s32[1024]{0:T(1024)S(1)} %get-tuple-element.30), kind=kCustom, calls=%fused_computation.2.clone | custom fusion | bytes 4720896 | tf_op jit(solution)/shard_map/jit(_take)/gather | solution.py:48
  39.1 4.0 %gather_fusion = f32[576]{0:T(1024)S(1)} fusion(f32[257]{0:T(512)S(1)} %pad_maximum_fusion.4, s32[1024]{0:T(1024)S(1)} %get-tuple-element.29), kind=kCustom, calls=%fused_computation.4 | custom fusion | bytes 6912 | tf_op jit(solution)/shard_map/jit(_take)/gather | solution.py:47
  43.1 3.8 %multiply_convert_fusion = bf16[576,2048]{1,0:T(8,128)(2,1)} fusion(bf16[576,2048]{1,0:T(8,128)(2,1)} %gather_fusion.3, f32[576]{0:T(1024)S(1)} %and_select_fusion, pred[576]{0:T(1024)(128)(4,1)S(1)} %get-tuple-element.19), kind=kLoop, calls=%fused_computation.9 | loop fusion | flops 4718592 | bytes 4721472 | tf_op jit(solution)/shard_map/convert_element_type | solution.py:51
  46.9 4.1 %reshape.174 = bf16[16,36,2048]{2,1,0:T(8,128)(2,1)} reshape(bf16[576,2048]{1,0:T(8,128)(2,1)} %multiply_convert_fusion) | data formatting | bytes 4718592 | tf_op jit(solution)/shard_map/reshape | solution.py:52
  51.0 43.4 %all-to-all-done = bf16[16,36,2048]{2,1,0:T(8,128)(2,1)} async-done(((bf16[16,36,2048]{2,1,0:T(8,128)(2,1)}), bf16[16,36,2048]{2,1,0:T(8,128)(2,1)}, u32[]{:S(2)}, u32[]{:S(2)}) %all-to-all-start) | async-done | bytes 2359328 | tf_op jit(solution)/shard_map/all_to_all | solution.py:55
  94.4 5.5 %all-to-all-start.2 = ((bf16[16,36,2048]{2,1,0:T(8,128)(2,1)}), bf16[16,36,2048]{2,1,0:T(8,128)(2,1)}, u32[]{:S(2)}, u32[]{:S(2)}) async-start(bf16[16,36,2048]{2,1,0:T(8,128)(2,1)} %reshape.174), calls=%async_computation.2 | async-start | bytes 5242880 | tf_op jit(solution)/shard_map/all_to_all | solution.py:74
  99.9 0.2 reduce-scatter.2.cloned.1.call-start
  100.2 3.3 constant_dynamic-update-slice_fusion.1
  103.5 1.5 constant_dynamic-update-slice_fusion
  105.0 4.1 %reshape.169 = bf16[576,2048]{1,0:T(8,128)(2,1)} reshape(bf16[16,36,2048]{2,1,0:T(8,128)(2,1)} %all-to-all-done) | data formatting | bytes 4718592 | tf_op jit(solution)/shard_map/reshape | solution.py:56
  109.1 6.9 %fusion.12 = f32[576,1024]{1,0:T(8,128)} fusion(bf16[576,2048]{1,0:T(8,128)(2,1)} %reshape.169, bf16[2048,1024]{1,0:T(8,128)(2,1)} %constant_dynamic-update-slice_fusion), kind=kOutput, calls=%fused_computation.58 | convolution fusion | flops 2415919104 | bytes 8912896 | tf_op jit(solution)/shard_map/dot_general | solution.py:57
  116.0 43.6 %all-to-all-done.2 = bf16[16,36,2048]{2,1,0:T(8,128)(2,1)} async-done(((bf16[16,36,2048]{2,1,0:T(8,128)(2,1)}), bf16[16,36,2048]{2,1,0:T(8,128)(2,1)}, u32[]{:S(2)}, u32[]{:S(2)}) %all-to-all-start.2) | async-done | bytes 2359328 | tf_op jit(solution)/shard_map/all_to_all | solution.py:74
  159.6 4.1 %reshape.175 = bf16[576,2048]{1,0:T(8,128)(2,1)} reshape(bf16[16,36,2048]{2,1,0:T(8,128)(2,1)} %all-to-all-done.2) | data formatting | bytes 4718592 | tf_op jit(solution)/shard_map/reshape | solution.py:75
  163.8 4.3 %multiply_convert_fusion.2 = (bf16[576,512]{1,0:T(8,128)(2,1)S(1)}, bf16[576,512]{1,0:T(8,128)(2,1)S(1)}, bf16[576,512]{1,0:T(8,128)(2,1)S(1)}) fusion(f32[576,1024]{1,0:T(8,128)} %fusion.12, bf16[576,2048]{1,0:T(8,128)(2,1)} %reshape.175, bf16[512,2048]{1,0:T(8,128)(2,1)S(1)} %copy-done), kind=kOutput, calls=%fused_computation.16 | convolution fusion | flops 1212383232 | bytes 8585216 | tf_op jit(solution)/shard_map/dot_general | solution.py:27
  168.1 1.9 fusion.13
  170.2 3.5 fusion.1
  173.6 7.2 %pad_maximum_fusion = f32[2048,1536]{0,1:T(8,128)} fusion(f32[2048,512]{0,1:T(8,128)S(1)} %fusion.13, f32[2048,1024]{0,1:T(8,128)S(1)} %fusion.1), kind=kLoop, calls=%fused_computation.6 | loop fusion | flops 3145728 | bytes 25165824 | tf_op jit(solution)/shard_map/concatenate | solution.py:95
  180.9 6.6 %convolution_convert_fusion.1 = bf16[576,2048]{1,0:T(8,128)(2,1)} fusion(bf16[2048,1024]{1,0:T(8,128)(2,1)} %constant_dynamic-update-slice_fusion, bf16[576,512]{1,0:T(8,128)(2,1)} %copy-done.7, bf16[576,512]{1,0:T(8,128)(2,1)} %copy-done.6), kind=kOutput, calls=%fused_computation.11 | convolution fusion | flops 2419458048 | bytes 7733248 | tf_op jit(solution)/shard_map/dot_general | solution.py:27
  187.5 4.1 %reshape.176 = bf16[16,36,2048]{2,1,0:T(8,128)(2,1)} reshape(bf16[576,2048]{1,0:T(8,128)(2,1)} %convolution_convert_fusion.1) | data formatting | bytes 4718592 | tf_op jit(solution)/shard_map/reshape | solution.py:82
  191.6 5.5 %all-to-all-start.3 = ((bf16[16,36,2048]{2,1,0:T(8,128)(2,1)}), bf16[16,36,2048]{2,1,0:T(8,128)(2,1)}, u32[]{:S(2)}, u32[]{:S(2)}) async-start(bf16[16,36,2048]{2,1,0:T(8,128)(2,1)} %reshape.176), calls=%async_computation.3 | async-start | bytes 5242880 | tf_op jit(solution)/shard_map/all_to_all | solution.py:83
  197.2 2.8 convolution_convert_fusion
  200.0 4.1 %reshape.170 = bf16[16,36,2048]{2,1,0:T(8,128)(2,1)} reshape(bf16[576,2048]{1,0:T(8,128)(2,1)} %convolution_convert_fusion) | data formatting | bytes 4718592 | tf_op jit(solution)/shard_map/reshape | solution.py:71
  204.1 52.7 %all-to-all-done.3 = bf16[16,36,2048]{2,1,0:T(8,128)(2,1)} async-done(((bf16[16,36,2048]{2,1,0:T(8,128)(2,1)}), bf16[16,36,2048]{2,1,0:T(8,128)(2,1)}, u32[]{:S(2)}, u32[]{:S(2)}) %all-to-all-start.3) | async-done | bytes 2359328 | tf_op jit(solution)/shard_map/all_to_all | solution.py:83
  256.9 5.5 %all-to-all-start.1 = ((bf16[16,36,2048]{2,1,0:T(8,128)(2,1)}), bf16[16,36,2048]{2,1,0:T(8,128)(2,1)}, u32[]{:S(2)}, u32[]{:S(2)}) async-start(bf16[16,36,2048]{2,1,0:T(8,128)(2,1)} %reshape.170), calls=%async_computation.1 | async-start | bytes 5242880 | tf_op jit(solution)/shard_map/all_to_all | solution.py:73
  262.4 4.1 %convert_reduce_fusion = f32[8,36,2048]{2,1,0:T(8,128)} fusion(bf16[16,36,2048]{2,1,0:T(8,128)(2,1)} %all-to-all-done.3), kind=kLoop, calls=%fused_computation.7 | loop fusion | flops 1769472 | bytes 4718592 | tf_op jit(solution)/shard_map/reduce_sum | solution.py:87
  266.6 2.9 reshape.177
  269.5 52.6 %all-to-all-done.1 = bf16[16,36,2048]{2,1,0:T(8,128)(2,1)} async-done(((bf16[16,36,2048]{2,1,0:T(8,128)(2,1)}), bf16[16,36,2048]{2,1,0:T(8,128)(2,1)}, u32[]{:S(2)}, u32[]{:S(2)}) %all-to-all-start.1) | async-done | bytes 2359328 | tf_op jit(solution)/shard_map/all_to_all | solution.py:73
  322.1 4.1 %convert_reduce_fusion.1 = f32[8,36,2048]{2,1,0:T(8,128)} fusion(bf16[16,36,2048]{2,1,0:T(8,128)(2,1)} %all-to-all-done.1), kind=kLoop, calls=%fused_computation.8 | loop fusion | flops 1769472 | bytes 4718592 | tf_op jit(solution)/shard_map/reduce_sum | solution.py:87
  326.2 2.9 reshape.171
  329.0 5.3 %gather_fusion.4 = f32[256,2048]{1,0:T(8,128)} fusion(f32[288,2048]{1,0:T(8,128)} %reshape.177, s32[1024]{0:T(1024)S(1)} %pad_clamp_fusion.1), kind=kCustom, calls=%fused_computation.3.clone | custom fusion | bytes 4195328 | tf_op jit(solution)/shard_map/jit(_take)/gather | solution.py:88
  334.4 5.3 %gather_fusion.2 = f32[256,2048]{1,0:T(8,128)} fusion(f32[288,2048]{1,0:T(8,128)} %reshape.171, s32[1024]{0:T(1024)S(1)} %pad_clamp_fusion.1), kind=kCustom, calls=%fused_computation.1.clone | custom fusion | bytes 4195328 | tf_op jit(solution)/shard_map/jit(_take)/gather | solution.py:88
  339.6 4.7 %broadcast_select_fusion.1 = (f32[256,2048]{1,0:T(8,128)}, f32[256,2048]{1,0:T(8,128)}) fusion(f32[256,2048]{1,0:T(8,128)} %gather_fusion.4, pred[256]{0:T(512)(128)(4,1)S(1)} %get-tuple-element.17, f32[256,2048]{1,0:T(8,128)} %gather_fusion.2, f32[256]{0:T(256)S(1)} %div.25), kind=kLoop, calls=%fused_computation.20 | loop fusion | flops 1572864 | bytes 8389888 | tf_op jit(solution)/shard_map/jit(_take)/select_n | solution.py:88
  344.4 3.5 reshape.178
  347.8 3.4 reshape.172
  351.3 5.0 %reduce_sum.52 = bf16[128,2048]{1,0:T(8,128)(2,1)} reduce(f32[128,2,2048]{2,1,0:T(2,128)} %reshape.178, f32[]{:T(128)} %constant.69.clone.1), dimensions={1}, to_apply=%region_7.10 | reduce | flops 262144 | bytes 2621444 | tf_op jit(solution)/shard_map/reduce_sum | solution.py:93
  356.3 5.0 %reduce_sum.50 = bf16[128,2048]{1,0:T(8,128)(2,1)} reduce(f32[128,2,2048]{2,1,0:T(2,128)} %reshape.172, f32[]{:T(128)} %constant.69.clone.1), dimensions={1}, to_apply=%region_5.8 | reduce | flops 262144 | bytes 2621444 | tf_op jit(solution)/shard_map/reduce_sum | solution.py:90
  361.2 1.9 slice_bitcast_fusion
  363.1 0.8 copy.19
  363.9 0.8 copy.18
  (44 shorter events, 1.8 us)
Async XLA Ops:
  7.2 156.6 %copy-start = (bf16[512,2048]{1,0:T(8,128)(2,1)S(1)}, bf16[512,2048]{1,0:T(8,128)(2,1)}, u32[]{:S(2)}) copy-start(bf16[512,2048]{1,0:T(8,128)(2,1)} %param.17) | copy-start | bytes 6291460
  24.6 10.1 %copy-start.5 = (s32[128,2]{0,1:T(2,128)S(1)}, s32[128,2]{0,1:T(2,128)}, u32[]{:S(2)}) copy-start(s32[128,2]{0,1:T(2,128)} %param.13) | copy-start | bytes 3076
  24.6 10.4 %copy-start.4 = (bf16[128,2048]{1,0:T(8,128)(2,1)S(1)}, bf16[128,2048]{1,0:T(8,128)(2,1)}, u32[]{:S(2)}) copy-start(bf16[128,2048]{1,0:T(8,128)(2,1)} %param.14) | copy-start | bytes 1572868
  24.6 69.8 %all-to-all-start = ((bf16[16,36,2048]{2,1,0:T(8,128)(2,1)}), bf16[16,36,2048]{2,1,0:T(8,128)(2,1)}, u32[]{:S(2)}, u32[]{:S(2)}) async-start(bf16[16,36,2048]{2,1,0:T(8,128)(2,1)} %reshape.168), calls=%async_computation | async-start | bytes 5242880 | tf_op jit(solution)/shard_map/all_to_all | solution.py:55
  94.4 65.2 %all-to-all-start.2 = ((bf16[16,36,2048]{2,1,0:T(8,128)(2,1)}), bf16[16,36,2048]{2,1,0:T(8,128)(2,1)}, u32[]{:S(2)}, u32[]{:S(2)}) async-start(bf16[16,36,2048]{2,1,0:T(8,128)(2,1)} %reshape.174), calls=%async_computation.2 | async-start | bytes 5242880 | tf_op jit(solution)/shard_map/all_to_all | solution.py:74
  99.9 261.3 %reduce-scatter.2.cloned.1.call-start = ((), (), s32[]{:S(2)}) async-start(), calls=%async_computation.5 | async-start | bytes 13369344 | tf_op jit(solution)/shard_map/reduce_scatter | solution.py:94
  100.2 3.3 copy-start.3
  163.8 4.3 %copy-start.2 = (bf16[576,2048]{1,0:T(8,128)(2,1)S(1)}, bf16[576,2048]{1,0:T(8,128)(2,1)}, u32[]{:S(2)}) copy-start(bf16[576,2048]{1,0:T(8,128)(2,1)} %reshape.175) | copy-start | bytes 7077892
  168.0 1.9 copy-start.6
  168.1 1.9 copy-start.7
  168.1 2.1 copy-start.1
  191.6 65.2 %all-to-all-start.3 = ((bf16[16,36,2048]{2,1,0:T(8,128)(2,1)}), bf16[16,36,2048]{2,1,0:T(8,128)(2,1)}, u32[]{:S(2)}, u32[]{:S(2)}) async-start(bf16[16,36,2048]{2,1,0:T(8,128)(2,1)} %reshape.176), calls=%async_computation.3 | async-start | bytes 5242880 | tf_op jit(solution)/shard_map/all_to_all | solution.py:83
  256.9 65.2 %all-to-all-start.1 = ((bf16[16,36,2048]{2,1,0:T(8,128)(2,1)}), bf16[16,36,2048]{2,1,0:T(8,128)(2,1)}, u32[]{:S(2)}, u32[]{:S(2)}) async-start(bf16[16,36,2048]{2,1,0:T(8,128)(2,1)} %reshape.170), calls=%async_computation.1 | async-start | bytes 5242880 | tf_op jit(solution)/shard_map/all_to_all | solution.py:73
Sparse Core Ops, SparseCore 0:
  181.0 98.5 reduce-scatter.1
where the time goes:
time: 373 us; the launch traced here: 372 us
  waiting for transfers between devices  192 us (51%)
  local copies, waits for them, and re-layouts  73.1 us (20%)
  other arithmetic  38.9 us (10%)
  starting transfers between devices  26.9 us (7%)
  matrix products  26 us (7%)
  between operations  14.3 us (4%)
    all_to_all x1, waiting for transfers between devices, per_device(): lax.all_to_all(dx, 'expert', split_axis=0, concat_axis=0, tiled=True)  52.7 us
    all_to_all x1, waiting for transfers between devices, per_device(): lax.all_to_all(z, 'expert', split_axis=0, concat_axis=0, tiled=True)  52.6 us
    all_to_all x1, waiting for transfers between devices, per_device(): lax.all_to_all(dz_send, 'expert', split_axis=0, concat_axis=0, tiled=True)  43.6 us
    all_to_all x1, waiting for transfers between devices, per_device(): lax.all_to_all(x_send, 'expert', split_axis=0, concat_axis=0, tiled=True)  43.4 us
    dot_general x2, matrix products, contract_cols(): lax.dot_general(left, right, (((1,), (1,)), ((), ())), preferred_element_...  10.9 us
    gather x2, local copies, waits for them, and re-layouts, combine(): return jnp.take(summed.reshape(EXPERTS * CAP, width), pair_slot, axis=0)  10.6 us
    all_to_all x1, starting transfers between devices, per_device(): lax.all_to_all(x_send, 'expert', split_axis=0, concat_axis=0, tiled=True)  10.1 us
    reduce_sum x2, other arithmetic, combine(): jnp.sum(back.reshape(EXPERTS, tiles, CAP, width).astype(jnp.float32), axi...  8.21 us
  transfers between devices with their start and end apart: 5, of which 4 were waited for; matrix products, arithmetic and copies ran while one was open for 26% of the time, Pallas kernels for 0%

commit v1 on v0

v1 whole, which is shorter than its diff:
```python
import jax
import jax.numpy as jnp
from jax import lax
from jax.experimental import pallas as pl
from jax.experimental.pallas import tpu as pltpu
from jax.sharding import PartitionSpec as P

MESH = pl.DeviceIdType.MESH
BF16 = jnp.bfloat16
F32 = jnp.float32

T = 128
D = 2048
H = 512
E = 8
MAIN = 32
REM = 4
W = 512
J = D // W
BLK = J * MAIN + J * REM
ROWS = 2 * E * (MAIN + REM)
HALF = 80
Q = 384


def dot(a, b):
    return jnp.dot(a, b, preferred_element_type=F32)


def dot_rows(a, b):
    return lax.dot_general(a, b, (((0,), (0,)), ((), ())), preferred_element_type=F32)


def dot_cols(a, b):
    return lax.dot_general(a, b, (((1,), (1,)), ((), ())), preferred_element_type=F32)


def kernel(
    routes,
    gates,
    tokens,
    cotangent,
    w_gate,
    w_up,
    w_down,
    mixed,
    input_grad,
    grad_gate,
    grad_up,
    grad_down,
    wgu,
    wd,
    gx,
    gxr,
    gf,
    gfr,
    perm,
    send,
    xr,
    zr,
    back,
    relay_a,
    relay_b,
    xrows,
    dzrows,
    act_s,
    dact_s,
    h_s,
    bg,
    own_s,
    part_out,
    part_in,
    g_s,
    a_recv,
    a_send,
    a_tot,
    b_recv,
    b_send,
    load_sem,
    local_sem,
    ssem,
    rsem,
):
    dp = lax.axis_index("dp")
    ex = lax.axis_index("expert")
    z, core = ex // 2, ex % 2
    x, y = dp // 4, dp % 4

    def zz(d):
        return (z + d + 8) % 8

    def zdev(d):
        return (dp, zz(d) * 2 + core)

    partner = (dp, z * 2 + (1 - core))

    def ring_dev(along_x, d):
        if along_x:
            return (((x + d + 4) % 4) * 4 + y, ex)
        return (x * 4 + (y + d + 4) % 4, ex)

    barrier = pltpu.get_barrier_semaphore()
    peers = [zdev(d) for d in range(1, 8)] + [partner]
    peers += [ring_dev(True, 1), ring_dev(True, -1), ring_dev(False, 1), ring_dev(False, -1)]
    for peer in peers:
        pl.semaphore_signal(barrier, inc=1, device_id=peer, device_id_type=MESH)

    loads = [
        pltpu.make_async_copy(w_gate, wgu.at[:, pl.ds(0, H)], load_sem.at[0]),
        pltpu.make_async_copy(w_up, wgu.at[:, pl.ds(H, H)], load_sem.at[1]),
        pltpu.make_async_copy(w_down, wd, load_sem.at[2]),
    ]
    for load in loads:
        load.start()

    row16 = lax.broadcasted_iota(jnp.int32, (16, T), 0)
    first = row16 == routes[0:1, :]
    second = row16 == routes[1:2, :]
    named = jnp.logical_or(first, second)
    earlier = lax.broadcasted_iota(jnp.int32, (T, T), 0) < lax.broadcasted_iota(jnp.int32, (T, T), 1)
    before = dot(
        jnp.where(named, 1.0, 0.0).astype(BF16), jnp.where(earlier, 1.0, 0.0).astype(BF16)
    ).astype(jnp.int32)
    slot = jnp.where(named, before, -1)
    gate = jnp.where(first, gates[0:1, :], 0) + jnp.where(second, gates[1:2, :], 0)
    high = ((gate >> 3) << 3).astype(F32) * (1.0 / 1024.0)
    low = (gate & 7).astype(F32) * (1.0 / 1024.0)
    rowm = lax.broadcasted_iota(jnp.int32, (MAIN, T), 0)
    rowr = lax.broadcasted_iota(jnp.int32, (J * REM, T), 0)
    for e in range(E):
        at = slot[e : e + 1, :]
        hi, lo = high[e : e + 1, :], low[e : e + 1, :]
        hit = rowm == at
        gx[pl.ds(e * MAIN, MAIN), :] = jnp.where(hit, 1.0, 0.0).astype(BF16)
        gf[pl.ds(e * MAIN, MAIN), pl.ds(0, T)] = jnp.where(hit, hi, 0.0).astype(BF16)
        gf[pl.ds(e * MAIN, MAIN), pl.ds(T, T)] = jnp.where(hit, lo, 0.0).astype(BF16)
        hitr = (MAIN + (rowr & (REM - 1))) == at
        for j in range(J):
            hitj = jnp.logical_and(hitr, (rowr >> 2) == j)
            rows = pl.ds(e * J * REM, J * REM)
            gxr[j, rows, :] = jnp.where(hitj, 1.0, 0.0).astype(BF16)
            gfr[j, rows, pl.ds(0, T)] = jnp.where(hitj, hi, 0.0).astype(BF16)
            gfr[j, rows, pl.ds(T, T)] = jnp.where(hitj, lo, 0.0).astype(BF16)
    pr = lax.broadcasted_iota(jnp.int32, (E * REM, E * J * REM), 0)
    pc = lax.broadcasted_iota(jnp.int32, (E * REM, E * J * REM), 1)
    for j in range(J):
        same = jnp.logical_and(pr >> 2 == pc >> 4, (pc & 15) == j * REM + (pr & 3))
        perm[j] = jnp.where(same, 1.0, 0.0).astype(BF16)

    def cols(j):
        return pl.ds(pl.multiple_of(j * W, W), W)

    def main_rows(j):
        return pl.ds(pl.multiple_of(j * MAIN, MAIN), MAIN)

    def pack(buf, j, rows):
        buf[:, main_rows(j), :] = rows.reshape(E, MAIN, W)

    def pack_rest(buf, rest):
        buf[:, pl.ds(J * MAIN, J * REM), :] = rest.astype(BF16).reshape(E, J * REM, W)

    def rest_of(buf):
        return buf[:, pl.ds(J * MAIN, J * REM), :].reshape(E * J * REM, W)

    def gather_x(j, rest):
        piece = tokens[:, cols(j)]
        pack(send.at[0], j, dot(gx[...], piece).astype(BF16))
        return rest + dot(gxr[j], piece)

    def gather_dz(j, rest):
        piece = cotangent[:, cols(j)]
        both = jnp.concatenate([piece, piece], axis=0)
        pack(send.at[1], j, dot(gf[...], both).astype(BF16))
        return rest + dot(gfr[j], both)

    zero_rest = jnp.zeros((E * J * REM, W), F32)

    def remote(src, dst, index, device):
        return pltpu.make_async_remote_copy(
            src_ref=src,
            dst_ref=dst,
            send_sem=ssem.at[index],
            recv_sem=rsem.at[index],
            device_id=device,
            device_id_type=MESH,
        )

    started = []

    def start(copies):
        for copy in copies:
            copy.start()
            started.append(copy)

    class Exchange:
        def __init__(self, k, recv):
            src, ra, rb = send.at[k], relay_a.at[k], relay_b.at[k]
            base = 10 * k
            far = zz(4)
            upper, lower = pl.ds(0, HALF), pl.ds(HALF, BLK - HALF)
            self.legs = [
                remote(src.at[far, upper], ra, base, zdev(2)),
                remote(src.at[far, lower], rb, base + 1, zdev(-2)),
            ]
            self.direct = [
                remote(src.at[zz(d)], recv.at[z], base + 2 + n, zdev(d))
                for n, d in enumerate((3, -3, 2, -2, 1, -1))
            ]
            self.onward = [
                remote(ra, recv.at[zz(-2), upper], base + 8, zdev(2)),
                remote(rb, recv.at[zz(2), lower], base + 9, zdev(-2)),
            ]
            self.own = pltpu.make_async_copy(src.at[z], recv.at[z], local_sem.at[k])

        def begin(self):
            start(self.legs)
            start(self.direct)
            self.own.start()

        def pass_on(self):
            for leg, copy in zip(self.legs, self.onward):
                leg.wait_recv()
                start([copy])

        def arrived(self):
            for copy in self.direct + self.onward:
                copy.wait_recv()
            self.own.wait()

    def unpack(got, rows):
        for g in range(2):

            def one(j, carry):
                rows[pl.ds(g * E * MAIN, E * MAIN), cols(j)] = got[g, :, main_rows(j), :].reshape(
                    E * MAIN, W
                )
                rest = dot(perm[j], rest_of(got.at[g])).astype(BF16)
                rows[pl.ds(2 * E * MAIN + g * E * REM, E * REM), cols(j)] = rest
                return carry

            lax.fori_loop(0, J, one, 0)

    om, orr = pl.ds(0, E * MAIN), pl.ds(E * MAIN, E * REM)

    def partials(k, product):
        def one(j, rest):
            value = product(j)
            n = E * MAIN
            pack(part_out.at[k], j, value[n : 2 * n].astype(BF16))
            own_s[om, cols(j)] = value[0:n]
            own_s[orr, cols(j)] = value[2 * n : 2 * n + E * REM]
            return rest + dot_rows(perm[j], value[2 * n + E * REM :].astype(BF16))

        pack_rest(part_out.at[k], lax.fori_loop(0, J, one, zero_rest))
        swap = remote(part_out.at[k], part_in.at[k], 42 + k, partner)
        start([swap])
        return swap

    def add_partials(k, to):
        def one(j, rest):
            got = part_in[k, :, main_rows(j), :].reshape(E * MAIN, W).astype(F32)
            pack(send.at[to], j, (own_s[om, cols(j)] + got).astype(BF16))
            more = own_s[orr, cols(j)] + dot(perm[j], rest_of(part_in.at[k]))
            return rest + dot_rows(perm[j], more.astype(BF16))

        pack_rest(send.at[to], lax.fori_loop(0, J, one, zero_rest))

    ex_x, ex_dz = Exchange(0, xr.at[0]), Exchange(1, zr.at[0])
    ex_z, ex_dx = Exchange(2, back.at[0]), Exchange(3, back.at[1])

    pack_rest(send.at[0], lax.fori_loop(0, J, gather_x, zero_rest))
    pl.semaphore_wait(barrier, len(peers))
    ex_x.begin()
    pack_rest(send.at[1], lax.fori_loop(0, J, gather_dz, zero_rest))
    ex_x.pass_on()
    ex_dz.begin()
    ex_x.arrived()
    swap_x = remote(xr.at[0], xr.at[1], 40, partner)
    start([swap_x])
    for load in loads:
        load.wait()
    swap_x.wait_recv()

    unpack(xr, xrows)

    def forward(n, carry):
        at = pl.ds(pl.multiple_of(n * 256, 256), 256)
        upat = pl.ds(pl.multiple_of(H + n * 256, 256), 256)
        a = dot(xrows[...], wgu[:, at])
        b = dot(xrows[...], wgu[:, upat])
        sig = jax.nn.sigmoid(a)
        act = a * sig
        h_s[:, at] = (act * b).astype(BF16)
        act_s[:, at] = act
        dact_s[:, at] = b * (sig * (1.0 + a * (1.0 - sig)))
        return carry

    lax.fori_loop(0, H // 256, forward, 0)
    swap = partials(0, lambda j: dot(h_s[...], wd[:, cols(j)]))
    ex_dz.pass_on()
    swap.wait_recv()
    add_partials(0, 2)
    ex_z.begin()

    ex_dz.arrived()
    swap_dz = remote(zr.at[0], zr.at[1], 41, partner)
    start([swap_dz])
    ex_z.pass_on()
    swap_dz.wait_recv()
    unpack(zr, dzrows)

    def backward(n, carry):
        at = pl.ds(pl.multiple_of(n * 256, 256), 256)
        upat = pl.ds(pl.multiple_of(H + n * 256, 256), 256)
        dh = dot_cols(dzrows[...], wd[at, :])
        bg[:, at] = (dh * dact_s[:, at]).astype(BF16)
        bg[:, upat] = (dh * act_s[:, at]).astype(BF16)
        return carry

    lax.fori_loop(0, H // 256, backward, 0)

    def grads(p, carry):
        at = pl.ds(pl.multiple_of(p * 256, 256), 256)
        both = dot_rows(xrows[:, at], bg[...]).astype(BF16)
        down = dot_rows(dzrows[:, at], h_s[...]).astype(BF16)
        px, py = p // 2, (p % 2) * 2
        for i in range(2):
            rows = slice(i * 128, (i + 1) * 128)
            g_s[0, px, py + i] = both[rows, 0:Q]
            g_s[1, px, py + i] = both[rows, Q : 2 * Q]
            g_s[2, px, py + i, :, pl.ds(0, 256)] = both[rows, 2 * Q : 1024]
            g_s[2, px, py + i, :, pl.ds(256, 128)] = down[rows, 0:128]
            g_s[3, px, py + i] = down[rows, 128:512]
        return carry

    lax.fori_loop(0, 8, grads, 0)

    class Ring:
        def __init__(self, k, along_x, part, recv, out):
            self.recv, self.part, self.out = recv, part, out
            self.me = x if along_x else y
            base = 44 + 6 * k
            right, left = ring_dev(along_x, 1), ring_dev(along_x, -1)
            self.legs = [
                remote(part(0, self.at(2)), recv.at[0], base, right),
                remote(part(1, self.at(2)), recv.at[1], base + 1, left),
            ]
            self.direct = [
                remote(part(1, self.at(1)), recv.at[2], base + 2, right),
                remote(part(0, self.at(-1)), recv.at[3], base + 3, left),
            ]
            self.sums = [
                remote(out.at[0], recv.at[4], base + 4, right),
                remote(out.at[1], recv.at[5], base + 5, left),
            ]

        def at(self, d):
            return (self.me + d + 4) % 4

        def begin(self):
            start(self.legs)
            start(self.direct)

        def relay(self):
            for side, d in ((0, 1), (1, -1)):
                self.legs[side].wait_recv()
                mine = self.part(side, self.at(d))[...].astype(F32)
                self.out[side] = (mine + self.recv[side].astype(F32)).astype(BF16)
                start([self.sums[side]])

        def total(self, side):
            mine = self.part(side, self.me)[...].astype(F32)
            other = self.recv[3 - side].astype(F32)
            return mine + other + self.recv[4 + side].astype(F32)

        def arrived(self):
            for copy in self.direct + self.sums:
                copy.wait_recv()

    ring_a = [
        Ring(0, True, lambda s, p: g_s.at[s, p], a_recv.at[0], a_send.at[0]),
        Ring(1, False, lambda s, p: g_s.at[2 + s, :, p], a_recv.at[1], a_send.at[1]),
    ]
    ring_b = [
        Ring(2, False, lambda s, p: a_tot.at[0, s, p], b_recv.at[0], b_send.at[0]),
        Ring(3, True, lambda s, p: a_tot.at[1, s, p], b_recv.at[1], b_send.at[1]),
    ]
    for ring in ring_a:
        ring.begin()

    swap = partials(1, lambda j: dot_cols(bg[...], wgu[cols(j), :]))
    for ring in ring_a:
        ring.relay()
    swap.wait_recv()
    add_partials(1, 3)
    ex_dx.begin()

    def combine(k, out, left, rest_left):
        def one(j, carry):
            rows = back[k, :, main_rows(j), :].reshape(E * MAIN, W)
            value = dot_rows(left[...], rows) + dot_rows(rest_left[j], rest_of(back.at[k]))
            if left.shape[1] == 2 * T:
                value = value[0:T] + value[T:]
            out[:, cols(j)] = value.astype(BF16)
            return carry

        lax.fori_loop(0, J, one, 0)

    ex_z.arrived()
    combine(0, mixed, gf, gfr)
    ex_dx.pass_on()

    for k, ring in enumerate(ring_a):
        ring.arrived()
        for side in range(2):
            a_tot[k, side] = ring.total(side).astype(BF16)
        ring_b[k].begin()
    for ring in ring_b:
        ring.relay()
    quarters = []
    for ring in ring_b:
        ring.arrived()
        quarters += [ring.total(0), ring.total(1)]
    q0, q1, q2, q3 = quarters
    grad_gate[:, pl.ds(0, Q)] = q0
    grad_gate[:, pl.ds(Q, H - Q)] = q1[:, 0:128]
    grad_up[:, pl.ds(0, 256)] = q1[:, 128:Q]
    grad_up[:, pl.ds(256, 256)] = q2[:, 0:256]
    grad_down[pl.ds(0, 128), :] = q2[:, 256:Q].T
    grad_down[pl.ds(128, Q), :] = q3.T

    ex_dx.arrived()
    combine(1, input_grad, gx, gxr)
    for copy in started:
        copy.wait_send()


def per_device(tokens, routes, gates, cotangent, w_gate, w_up, w_down):
    vmem = pl.BlockSpec(memory_space=pltpu.VMEM)
    hbm = pl.BlockSpec(memory_space=pl.ANY)
    half = (4, 128, Q)
    return pl.pallas_call(
        kernel,
        out_shape=(
            jax.ShapeDtypeStruct((T, D), BF16),
            jax.ShapeDtypeStruct((T, D), BF16),
            jax.ShapeDtypeStruct((128, H), F32),
            jax.ShapeDtypeStruct((128, H), F32),
            jax.ShapeDtypeStruct((H, 128), F32),
        ),
        in_specs=[vmem] * 4 + [hbm] * 3,
        out_specs=(vmem,) * 5,
        scratch_shapes=[
            pltpu.VMEM((D, 2 * H), BF16),
            pltpu.VMEM((H, D), BF16),
            pltpu.VMEM((E * MAIN, T), BF16),
            pltpu.VMEM((J, E * J * REM, T), BF16),
            pltpu.VMEM((E * MAIN, 2 * T), BF16),
            pltpu.VMEM((J, E * J * REM, 2 * T), BF16),
            pltpu.VMEM((J, E * REM, E * J * REM), BF16),
            pltpu.VMEM((4, E, BLK, W), BF16),
            pltpu.VMEM((2, E, BLK, W), BF16),
            pltpu.VMEM((2, E, BLK, W), BF16),
            pltpu.VMEM((2, E, BLK, W), BF16),
            pltpu.VMEM((4, HALF, W), BF16),
            pltpu.VMEM((4, BLK - HALF, W), BF16),
            pltpu.VMEM((ROWS, D), BF16),
            pltpu.VMEM((ROWS, D), BF16),
            pltpu.VMEM((ROWS, H), F32),
            pltpu.VMEM((ROWS, H), F32),
            pltpu.VMEM((ROWS, H), BF16),
            pltpu.VMEM((ROWS, 2 * H), BF16),
            pltpu.VMEM((E * (MAIN + REM), D), F32),
            pltpu.VMEM((2, E, BLK, W), BF16),
            pltpu.VMEM((2, E, BLK, W), BF16),
            pltpu.VMEM((4, 4, 4, 128, Q), BF16),
            pltpu.VMEM((2, 6) + half, BF16),
            pltpu.VMEM((2, 2) + half, BF16),
            pltpu.VMEM((2, 2) + half, BF16),
            pltpu.VMEM((2, 6, 128, Q), BF16),
            pltpu.VMEM((2, 2, 128, Q), BF16),
            pltpu.SemaphoreType.DMA((3,)),
            pltpu.SemaphoreType.DMA((4,)),
            pltpu.SemaphoreType.DMA((68,)),
            pltpu.SemaphoreType.DMA((68,)),
        ],
        compiler_params=pltpu.CompilerParams(
            collective_id=0, has_side_effects=True, vmem_limit_bytes=63_000_000
        ),
        name="moe",
    )(routes.T, gates.T, tokens, cotangent, w_gate, w_up, w_down)


def solution(mesh):
    in_specs = (
        P(("dp", "expert"), None),
        P(("dp", "expert"), None),
        P(("dp", "expert"), None),
        P(("dp", "expert"), None),
        P(None, "expert"),
        P(None, "expert"),
        P("expert", None),
    )
    out_specs = (
        P(("dp", "expert"), None),
        P(("dp", "expert"), None),
        P("dp", "expert"),
        P("dp", "expert"),
        P("expert", "dp"),
    )
    return jax.shard_map(
        per_device, mesh=mesh, in_specs=in_specs, out_specs=out_specs, check_vma=False
    )
```

time: 373 us -> 127 us (0.34)
  waiting for transfers between devices: 192 us -> 0 us
  Pallas kernels: 0 us -> 120 us
  local copies, waits for them, and re-layouts: 73.1 us -> 5.95 us
  other arithmetic: 38.9 us -> 0 us
  starting transfers between devices: 26.9 us -> 0 us
  matrix products: 26 us -> 0 us
  between operations: 14.3 us -> 0.67 us
    all_to_all x4 -> x0, waiting for transfers between devices: 192 us -> none  [the longest x1 52.7 us: per_device(): lax.all_to_all(dx, 'expert', split_axis=0, concat_axis=0, tiled=True)]
    pallas_call x0 -> x1, Pallas kernels: none -> 120 us  [per_device(): pl.pallas_call(kernel, out_shape=(jax.ShapeDtypeStruct((T, D), BF16), jax...]
    reshape x12 -> x0, local copies, waits for them, and re-layouts: 37.6 us -> none  [the longest x2 5.75 us: combine(): return jnp.take(summed.reshape(EXPERTS * CAP, width), pair_slot, axis=0)]
    all_to_all x4 -> x0, starting transfers between devices: 26.7 us -> none  [the longest x1 10.1 us: per_device(): lax.all_to_all(x_send, 'expert', split_axis=0, concat_axis=0, tiled=True)]
    dot_general x6 -> x0, matrix products: 26 us -> none  [the longest x2 10.9 us: contract_cols(): lax.dot_general(left, right, (((1,), (1,)), ((), ())), preferred_element_...]
    gather x5 -> x0, local copies, waits for them, and re-layouts: 22.6 us -> none  [the longest x2 10.6 us: combine(): return jnp.take(summed.reshape(EXPERTS * CAP, width), pair_slot, axis=0)]
    reduce_sum x5 -> x0, other arithmetic: 18.2 us -> none  [the longest x2 8.21 us: combine(): jnp.sum(back.reshape(EXPERTS, tiles, CAP, width).astype(jnp.float32), axi...]
    select_n x5 -> x0, other arithmetic: 8.1 us -> none  [the longest x1 4.72 us: combine(): return jnp.take(summed.reshape(EXPERTS * CAP, width), pair_slot, axis=0)]
  transfers between devices with their start and end apart: 5 -> 0, of which waited for: 4 -> 0; matrix products, arithmetic and copies ran while one was open for 26% -> 0% of each run, Pallas kernels for 0% -> 0%
where the time goes in v1:
time: 127 us; the launch traced here: 126 us
  Pallas kernels  120 us (94%)
  local copies, waits for them, and re-layouts  5.95 us (5%)
    pallas_call x1, Pallas kernels, per_device(): pl.pallas_call(kernel, out_shape=(jax.ShapeDtypeStruct((T, D), BF16), jax...  120 us
    unnamed x11, local copies, waits for them, and re-layouts  5.95 us

profile of v1, /device:TPU:1, one launch (start us, length us, event | category | flops | bytes accessed | tf_op | source)
XLA Modules:
  0.0 126.1 jit_solution(16174035214234698217)
XLA Ops:
  0.6 119.5 %moe.1 = (bf16[128,2048]{1,0:T(8,128)(2,1)}, bf16[128,2048]{1,0:T(8,128)(2,1)}, f32[128,512]{1,0:T(8,128)}, f32[128,512]{1,0:T(8,128)}, f32[512,128]{1,0:T(8,128)}) custom-call(s32[2,128]{1,0:T(2,128)} %bitcast.2, s32[2,128]{1,0:T(2,128)} %bitcast.3, bf16[128,2048]{1,0:T(8,128)(2,1)} %tokens.1, bf16[128,2048]{1,0:T(8,128)(2,1)} %cotangent.1, ...), custom_call_target="tpu_custom_call" | custom-call | tf_op jit(solution)/shard_map/moe/pallas_call | solution.py:442
  120.2 0.0 copy-start.2
  120.2 0.0 copy-start.1
  120.2 0.0 copy-start
  120.2 1.9 %copy.17 = bf16[128,2048]{1,0:T(8,128)(2,1)} copy(bf16[128,2048]{1,0:T(8,128)(2,1)} %get-tuple-element.10) | data formatting | bytes 1048576
  122.1 1.9 %copy.18 = bf16[128,2048]{1,0:T(8,128)(2,1)} copy(bf16[128,2048]{1,0:T(8,128)(2,1)} %get-tuple-element.11) | data formatting | bytes 1048576
  124.0 0.0 copy-done.2
  124.0 0.7 copy.19
  124.7 0.0 copy-done.1
  124.7 0.7 copy.20
  125.4 0.0 copy-done
  125.4 0.7 copy.21
Async XLA Ops:
  120.2 3.9 %copy-start.2 = (f32[128,512]{1,0:T(8,128)S(1)}, f32[128,512]{1,0:T(8,128)}, u32[]{:S(2)}) copy-start(f32[128,512]{1,0:T(8,128)} %get-tuple-element.12) | copy-start | bytes 786436
  120.2 4.6 %copy-start.1 = (f32[128,512]{1,0:T(8,128)S(1)}, f32[128,512]{1,0:T(8,128)}, u32[]{:S(2)}) copy-start(f32[128,512]{1,0:T(8,128)} %get-tuple-element.13) | copy-start | bytes 786436
  120.2 5.3 %copy-start = (f32[512,128]{1,0:T(8,128)S(1)}, f32[512,128]{1,0:T(8,128)}, u32[]{:S(2)}) copy-start(f32[512,128]{1,0:T(8,128)} %get-tuple-element.14) | copy-start | bytes 786436

commit v2 on v1

--- a/solution.py
+++ b/solution.py
@@ -19,7 +19,6 @@
 J = D // W
 BLK = J * MAIN + J * REM
 ROWS = 2 * E * (MAIN + REM)
-HALF = 80
 Q = 384
 
 
@@ -38,16 +37,26 @@
 def kernel(
     routes,
     gates,
-    tokens,
-    cotangent,
+    tokens_in,
+    cotangent_in,
     w_gate,
     w_up,
     w_down,
+    mixed_out,
+    dx_back,
+    left_out,
+    left_rest_out,
+    grad_gate_out,
+    grad_up_out,
+    grad_down_out,
+    tokens,
+    cotangent,
     mixed,
-    input_grad,
     grad_gate,
     grad_up,
     grad_down,
+    left,
+    left_rest,
     wgu,
     wd,
     gx,
@@ -59,8 +68,6 @@
     xr,
     zr,
     back,
-    relay_a,
-    relay_b,
     xrows,
     dzrows,
     act_s,
@@ -77,6 +84,7 @@
     b_recv,
     b_send,
     load_sem,
+    store_sem,
     local_sem,
     ssem,
     rsem,
@@ -105,12 +113,14 @@
     for peer in peers:
         pl.semaphore_signal(barrier, inc=1, device_id=peer, device_id_type=MESH)
 
+    load_x = pltpu.make_async_copy(tokens_in, tokens, load_sem.at[3])
+    load_dy = pltpu.make_async_copy(cotangent_in, cotangent, load_sem.at[4])
     loads = [
         pltpu.make_async_copy(w_gate, wgu.at[:, pl.ds(0, H)], load_sem.at[0]),
         pltpu.make_async_copy(w_up, wgu.at[:, pl.ds(H, H)], load_sem.at[1]),
         pltpu.make_async_copy(w_down, wd, load_sem.at[2]),
     ]
-    for load in loads:
+    for load in [load_x, load_dy] + loads:
         load.start()
 
     row16 = lax.broadcasted_iota(jnp.int32, (16, T), 0)
@@ -127,25 +137,35 @@
     low = (gate & 7).astype(F32) * (1.0 / 1024.0)
     rowm = lax.broadcasted_iota(jnp.int32, (MAIN, T), 0)
     rowr = lax.broadcasted_iota(jnp.int32, (J * REM, T), 0)
+    def hits(e, j):
+        if j is None:
+            return rowm == slot[e : e + 1, :]
+        hit = (MAIN + (rowr & (REM - 1))) == slot[e : e + 1, :]
+        return jnp.logical_and(hit, (rowr >> 2) == j)
+
     for e in range(E):
-        at = slot[e : e + 1, :]
-        hi, lo = high[e : e + 1, :], low[e : e + 1, :]
-        hit = rowm == at
-        gx[pl.ds(e * MAIN, MAIN), :] = jnp.where(hit, 1.0, 0.0).astype(BF16)
-        gf[pl.ds(e * MAIN, MAIN), pl.ds(0, T)] = jnp.where(hit, hi, 0.0).astype(BF16)
-        gf[pl.ds(e * MAIN, MAIN), pl.ds(T, T)] = jnp.where(hit, lo, 0.0).astype(BF16)
-        hitr = (MAIN + (rowr & (REM - 1))) == at
+        gx[pl.ds(e * MAIN, MAIN), :] = jnp.where(hits(e, None), 1.0, 0.0).astype(BF16)
         for j in range(J):
-            hitj = jnp.logical_and(hitr, (rowr >> 2) == j)
             rows = pl.ds(e * J * REM, J * REM)
-            gxr[j, rows, :] = jnp.where(hitj, 1.0, 0.0).astype(BF16)
-            gfr[j, rows, pl.ds(0, T)] = jnp.where(hitj, hi, 0.0).astype(BF16)
-            gfr[j, rows, pl.ds(T, T)] = jnp.where(hitj, lo, 0.0).astype(BF16)
-    pr = lax.broadcasted_iota(jnp.int32, (E * REM, E * J * REM), 0)
-    pc = lax.broadcasted_iota(jnp.int32, (E * REM, E * J * REM), 1)
-    for j in range(J):
-        same = jnp.logical_and(pr >> 2 == pc >> 4, (pc & 15) == j * REM + (pr & 3))
-        perm[j] = jnp.where(same, 1.0, 0.0).astype(BF16)
+            gxr[j, rows, :] = jnp.where(hits(e, j), 1.0, 0.0).astype(BF16)
+
+    def scaled_masks():
+        for e in range(E):
+            for n, part in enumerate((high[e : e + 1, :], low[e : e + 1, :])):
+                lanes = pl.ds(n * T, T)
+                gf[pl.ds(e * MAIN, MAIN), lanes] = jnp.where(hits(e, None), part, 0.0).astype(BF16)
+                for j in range(J):
+                    rows = pl.ds(e * J * REM, J * REM)
+                    gfr[j, rows, lanes] = jnp.where(hits(e, j), part, 0.0).astype(BF16)
+
+    def other_masks():
+        pr = lax.broadcasted_iota(jnp.int32, (E * REM, E * J * REM), 0)
+        pc = lax.broadcasted_iota(jnp.int32, (E * REM, E * J * REM), 1)
+        for j in range(J):
+            same = jnp.logical_and(pr >> 2 == pc >> 4, (pc & 15) == j * REM + (pr & 3))
+            perm[j] = jnp.where(same, 1.0, 0.0).astype(BF16)
+            left_rest[j] = gxr[j].astype(F32).T.astype(BF16)
+        left[...] = gx[...].astype(F32).T.astype(BF16)
 
     def cols(j):
         return pl.ds(pl.multiple_of(j * W, W), W)
@@ -194,36 +214,19 @@
 
     class Exchange:
         def __init__(self, k, recv):
-            src, ra, rb = send.at[k], relay_a.at[k], relay_b.at[k]
-            base = 10 * k
-            far = zz(4)
-            upper, lower = pl.ds(0, HALF), pl.ds(HALF, BLK - HALF)
-            self.legs = [
-                remote(src.at[far, upper], ra, base, zdev(2)),
-                remote(src.at[far, lower], rb, base + 1, zdev(-2)),
-            ]
-            self.direct = [
-                remote(src.at[zz(d)], recv.at[z], base + 2 + n, zdev(d))
-                for n, d in enumerate((3, -3, 2, -2, 1, -1))
-            ]
-            self.onward = [
-                remote(ra, recv.at[zz(-2), upper], base + 8, zdev(2)),
-                remote(rb, recv.at[zz(2), lower], base + 9, zdev(-2)),
+            src = send.at[k]
+            self.copies = [
+                remote(src.at[zz(d)], recv.at[z], 7 * k + n, zdev(d))
+                for n, d in enumerate((4, 3, -3, 2, -2, 1, -1))
             ]
             self.own = pltpu.make_async_copy(src.at[z], recv.at[z], local_sem.at[k])
 
         def begin(self):
-            start(self.legs)
-            start(self.direct)
+            start(self.copies)
             self.own.start()
 
-        def pass_on(self):
-            for leg, copy in zip(self.legs, self.onward):
-                leg.wait_recv()
-                start([copy])
-
         def arrived(self):
-            for copy in self.direct + self.onward:
+            for copy in self.copies:
                 copy.wait_recv()
             self.own.wait()
 
@@ -252,7 +255,7 @@
             return rest + dot_rows(perm[j], value[2 * n + E * REM :].astype(BF16))
 
         pack_rest(part_out.at[k], lax.fori_loop(0, J, one, zero_rest))
-        swap = remote(part_out.at[k], part_in.at[k], 42 + k, partner)
+        swap = remote(part_out.at[k], part_in.at[k], 30 + k, partner)
         start([swap])
         return swap
 
@@ -266,16 +269,25 @@
         pack_rest(send.at[to], lax.fori_loop(0, J, one, zero_rest))
 
     ex_x, ex_dz = Exchange(0, xr.at[0]), Exchange(1, zr.at[0])
-    ex_z, ex_dx = Exchange(2, back.at[0]), Exchange(3, back.at[1])
-
+    ex_z, ex_dx = Exchange(2, back), Exchange(3, dx_back)
+
+    load_x.wait()
     pack_rest(send.at[0], lax.fori_loop(0, J, gather_x, zero_rest))
     pl.semaphore_wait(barrier, len(peers))
     ex_x.begin()
+    scaled_masks()
+    load_dy.wait()
     pack_rest(send.at[1], lax.fori_loop(0, J, gather_dz, zero_rest))
-    ex_x.pass_on()
     ex_dz.begin()
+    other_masks()
+    stores = [
+        pltpu.make_async_copy(left, left_out, store_sem.at[0]),
+        pltpu.make_async_copy(left_rest, left_rest_out, store_sem.at[1]),
+    ]
+    for store in stores:
+        store.start()
     ex_x.arrived()
-    swap_x = remote(xr.at[0], xr.at[1], 40, partner)
+    swap_x = remote(xr.at[0], xr.at[1], 28, partner)
     start([swap_x])
     for load in loads:
         load.wait()
@@ -297,15 +309,13 @@
 
     lax.fori_loop(0, H // 256, forward, 0)
     swap = partials(0, lambda j: dot(h_s[...], wd[:, cols(j)]))
-    ex_dz.pass_on()
     swap.wait_recv()
     add_partials(0, 2)
     ex_z.begin()
 
     ex_dz.arrived()
-    swap_dz = remote(zr.at[0], zr.at[1], 41, partner)
+    swap_dz = remote(zr.at[0], zr.at[1], 29, partner)
     start([swap_dz])
-    ex_z.pass_on()
     swap_dz.wait_recv()
     unpack(zr, dzrows)
 
@@ -339,7 +349,7 @@
         def __init__(self, k, along_x, part, recv, out):
             self.recv, self.part, self.out = recv, part, out
             self.me = x if along_x else y
-            base = 44 + 6 * k
+            base = 32 + 6 * k
             right, left = ring_dev(along_x, 1), ring_dev(along_x, -1)
             self.legs = [
                 remote(part(0, self.at(2)), recv.at[0], base, right),
@@ -395,20 +405,20 @@
     add_partials(1, 3)
     ex_dx.begin()
 
-    def combine(k, out, left, rest_left):
-        def one(j, carry):
-            rows = back[k, :, main_rows(j), :].reshape(E * MAIN, W)
-            value = dot_rows(left[...], rows) + dot_rows(rest_left[j], rest_of(back.at[k]))
-            if left.shape[1] == 2 * T:
-                value = value[0:T] + value[T:]
-            out[:, cols(j)] = value.astype(BF16)
-            return carry
-
-        lax.fori_loop(0, J, one, 0)
+    def combine(j, carry):
+        rows = back[:, main_rows(j), :].reshape(E * MAIN, W)
+        value = dot_rows(gf[...], rows) + dot_rows(gfr[j], rest_of(back))
+        mixed[:, cols(j)] = (value[0:T] + value[T:]).astype(BF16)
+        return carry
+
+    def store(src, dst, n):
+        copy = pltpu.make_async_copy(src, dst, store_sem.at[n])
+        copy.start()
+        stores.append(copy)
 
     ex_z.arrived()
-    combine(0, mixed, gf, gfr)
-    ex_dx.pass_on()
+    lax.fori_loop(0, J, combine, 0)
+    store(mixed, mixed_out, 2)
 
     for k, ring in enumerate(ring_a):
         ring.arrived()
@@ -429,28 +439,117 @@
     grad_down[pl.ds(0, 128), :] = q2[:, 256:Q].T
     grad_down[pl.ds(128, Q), :] = q3.T
 
+    store(grad_gate, grad_gate_out, 3)
+    store(grad_up, grad_up_out, 4)
+    store(grad_down, grad_down_out, 5)
     ex_dx.arrived()
-    combine(1, input_grad, gx, gxr)
+    for copy in stores:
+        copy.wait()
     for copy in started:
         copy.wait_send()
+
+
+def finish(
+    dx_in,
+    left_in,
+    left_rest_in,
+    mixed_in,
+    grad_gate_in,
+    grad_up_in,
+    grad_down_in,
+    input_grad_out,
+    mixed_out,
+    grad_gate_out,
+    grad_up_out,
+    grad_down_out,
+    dx,
+    left,
+    left_rest,
+    input_grad,
+    mixed,
+    grad_gate,
+    grad_up,
+    grad_down,
+    in_sem,
+    out_sem,
+):
+    rest = pl.ds(J * MAIN, J * REM)
+    masks = [
+        pltpu.make_async_copy(left_in, left, in_sem.at[5]),
+        pltpu.make_async_copy(left_rest_in, left_rest, in_sem.at[6]),
+        pltpu.make_async_copy(dx_in.at[:, rest, :], dx.at[:, rest, :], in_sem.at[7]),
+    ]
+    pieces = []
+    for j in range(J):
+        rows = pl.ds(j * MAIN, MAIN)
+        pieces.append(pltpu.make_async_copy(dx_in.at[:, rows, :], dx.at[:, rows, :], in_sem.at[j]))
+    passed = [
+        (mixed_in, mixed, mixed_out),
+        (grad_gate_in, grad_gate, grad_gate_out),
+        (grad_up_in, grad_up, grad_up_out),
+        (grad_down_in, grad_down, grad_down_out),
+    ]
+    taken = [
+        pltpu.make_async_copy(src, mid, in_sem.at[8 + n]) for n, (src, mid, _) in enumerate(passed)
+    ]
+    given = [
+        pltpu.make_async_copy(mid, dst, out_sem.at[4 + n]) for n, (_, mid, dst) in enumerate(passed)
+    ]
+    for copy in masks + pieces + taken:
+        copy.start()
+    for take, give in zip(taken[0:1], given[0:1]):
+        take.wait()
+        give.start()
+    for copy in masks:
+        copy.wait()
+    cut = dx[:, rest, :].reshape(E * J * REM, W)
+    results = []
+    for j in range(J):
+        pieces[j].wait()
+        rows = dx[:, pl.ds(j * MAIN, MAIN), :].reshape(E * MAIN, W)
+        lanes = pl.ds(j * W, W)
+        input_grad[:, lanes] = (dot(left[...], rows) + dot(left_rest[j], cut)).astype(BF16)
+        result = pltpu.make_async_copy(
+            input_grad.at[:, lanes], input_grad_out.at[:, lanes], out_sem.at[j]
+        )
+        result.start()
+        results.append(result)
+        if j + 1 < len(taken):
+            taken[j + 1].wait()
+            given[j + 1].start()
+    for copy in given + results:
+        copy.wait()
 
 
 def per_device(tokens, routes, gates, cotangent, w_gate, w_up, w_down):
     vmem = pl.BlockSpec(memory_space=pltpu.VMEM)
     hbm = pl.BlockSpec(memory_space=pl.ANY)
     half = (4, 128, Q)
-    return pl.pallas_call(
+    outs = (
+        jax.ShapeDtypeStruct((T, D), BF16),
+        jax.ShapeDtypeStruct((128, H), F32),
+        jax.ShapeDtypeStruct((128, H), F32),
+        jax.ShapeDtypeStruct((H, 128), F32),
+    )
+    masks = (
+        jax.ShapeDtypeStruct((E, BLK, W), BF16),
+        jax.ShapeDtypeStruct((T, E * MAIN), BF16),
+        jax.ShapeDtypeStruct((J, T, E * J * REM), BF16),
+    )
+
+    def held(shapes):
+        return [pltpu.VMEM(s.shape, s.dtype) for s in shapes]
+
+    mixed, dx_back, left, left_rest, gate, up, down = pl.pallas_call(
         kernel,
-        out_shape=(
-            jax.ShapeDtypeStruct((T, D), BF16),
-            jax.ShapeDtypeStruct((T, D), BF16),
-            jax.ShapeDtypeStruct((128, H), F32),
-            jax.ShapeDtypeStruct((128, H), F32),
-            jax.ShapeDtypeStruct((H, 128), F32),
-        ),
-        in_specs=[vmem] * 4 + [hbm] * 3,
-        out_specs=(vmem,) * 5,
+        out_shape=outs[0:1] + masks + outs[1:],
+        in_specs=[vmem] * 2 + [hbm] * 5,
+        out_specs=(hbm,) * 7,
         scratch_shapes=[
+            pltpu.VMEM((T, D), BF16),
+            pltpu.VMEM((T, D), BF16),
+            *held(outs),
+            *held(masks[1:]),
             pltpu.VMEM((D, 2 * H), BF16),
             pltpu.VMEM((H, D), BF16),
             pltpu.VMEM((E * MAIN, T), BF16),
@@ -461,9 +560,7 @@
             pltpu.VMEM((4, E, BLK, W), BF16),
             pltpu.VMEM((2, E, BLK, W), BF16),
             pltpu.VMEM((2, E, BLK, W), BF16),
-            pltpu.VMEM((2, E, BLK, W), BF16),
-            pltpu.VMEM((4, HALF, W), BF16),
-            pltpu.VMEM((4, BLK - HALF, W), BF16),
+            pltpu.VMEM((E, BLK, W), BF16),
             pltpu.VMEM((ROWS, D), BF16),
             pltpu.VMEM((ROWS, D), BF16),
             pltpu.VMEM((ROWS, H), F32),
@@ -479,16 +576,32 @@
             pltpu.VMEM((2, 2) + half, BF16),
             pltpu.VMEM((2, 6, 128, Q), BF16),
             pltpu.VMEM((2, 2, 128, Q), BF16),
-            pltpu.SemaphoreType.DMA((3,)),
+            pltpu.SemaphoreType.DMA((5,)),
+            pltpu.SemaphoreType.DMA((6,)),
             pltpu.SemaphoreType.DMA((4,)),
-            pltpu.SemaphoreType.DMA((68,)),
-            pltpu.SemaphoreType.DMA((68,)),
+            pltpu.SemaphoreType.DMA((56,)),
+            pltpu.SemaphoreType.DMA((56,)),
         ],
         compiler_params=pltpu.CompilerParams(
             collective_id=0, has_side_effects=True, vmem_limit_bytes=63_000_000
         ),
         name="moe",
     )(routes.T, gates.T, tokens, cotangent, w_gate, w_up, w_down)
+    input_grad, mixed, gate, up, down = pl.pallas_call(
+        finish,
+        out_shape=outs[0:1] + outs,
+        in_specs=[hbm] * 7,
+        out_specs=(hbm,) * 5,
+        scratch_shapes=[
+            *held(masks),
+            *held(outs[0:1] + outs),
+            pltpu.SemaphoreType.DMA((12,)),
+            pltpu.SemaphoreType.DMA((8,)),
+        ],
+        compiler_params=pltpu.CompilerParams(vmem_limit_bytes=62_000_000),
+        name="finish",
+    )(dx_back, left, left_rest, mixed, gate, up, down)
+    return mixed, input_grad, gate, up, down
 
 
 def solution(mesh):

time: 127 us -> 123 us (0.969)
  local copies, waits for them, and re-layouts: 5.95 us -> 0 us
  Pallas kernels: 120 us -> 123 us
    unnamed x11 -> x0, local copies, waits for them, and re-layouts: 5.95 us -> none
    pallas_call x1 -> x2, Pallas kernels: 120 us -> 123 us  [the longest x1 119 us: per_device(): pl.pallas_call(kernel, out_shape=outs[0:1] + masks + outs[1:], in_specs=[...]
where the time goes in v2:
time: 123 us
  Pallas kernels  123 us (100%)
    pallas_call x1, Pallas kernels, per_device(): pl.pallas_call(kernel, out_shape=outs[0:1] + masks + outs[1:], in_specs=[...  119 us
    pallas_call x1, Pallas kernels, per_device(): pl.pallas_call(finish, out_shape=outs[0:1] + outs, in_specs=[hbm] * 7, ou...  3.25 us

profile of v2, /device:TPU:1, one launch (start us, length us, event | category | flops | bytes accessed | tf_op | source)
XLA Modules:
  0.0 123.3 jit_solution(6370385707078064013)
XLA Ops:
  0.6 119.4 %moe.1 = (bf16[128,2048]{1,0:T(8,128)(2,1)}, bf16[8,144,512]{2,1,0:T(8,128)(2,1)}, bf16[128,256]{1,0:T(8,128)(2,1)}, bf16[4,128,128]{2,1,0:T(8,128)(2,1)}, f32[1...) custom-call(s32[2,128]{1,0:T(2,128)} %bitcast.2, s32[2,128]{1,0:T(2,128)} %bitcast.3, ...), custom_call_target="tpu_custom_call" | custom-call | tf_op jit(solution)/shard_map/moe/pallas_call | solution.py:543
  120.1 3.2 %finish.1 = (bf16[128,2048]{1,0:T(8,128)(2,1)}, bf16[128,2048]{1,0:T(8,128)(2,1)}, f32[128,512]{1,0:T(8,128)}, f32[128,512]{1,0:T(8,128)}, f32[512,128]{1,0:T(8,128)}) custom-call(bf16[8,144,512]{2,1,0:T(8,128)(2,1)} %get-tuple-element.17.dx_in, bf16[128,256]{1,0:T(8,128)(2,1)} %get-tuple-element.18.left_in, ...), custom_call_target="tpu_custom_call" | custom-call | tf_op jit(solution)/shard_map/finish/pallas_call | solution.py:590

commit v3 on v2

--- a/solution.py
+++ b/solution.py
@@ -88,6 +88,8 @@
     local_sem,
     ssem,
     rsem,
+    ring_sem,
+    near_sem,
 ):
     dp = lax.axis_index("dp")
     ex = lax.axis_index("expert")
@@ -108,10 +110,19 @@
         return (x * 4 + (y + d + 4) % 4, ex)
 
     barrier = pltpu.get_barrier_semaphore()
-    peers = [zdev(d) for d in range(1, 8)] + [partner]
-    peers += [ring_dev(True, 1), ring_dev(True, -1), ring_dev(False, 1), ring_dev(False, -1)]
-    for peer in peers:
-        pl.semaphore_signal(barrier, inc=1, device_id=peer, device_id_type=MESH)
+    ring_peers = [zdev(d) for d in range(1, 8)]
+    near = [partner, ring_dev(True, 1), ring_dev(True, -1), ring_dev(False, 1), ring_dev(False, -1)]
+    first_member = z == 0
+
+    def signal(sem, devices):
+        for device in devices:
+            pl.semaphore_signal(sem, inc=1, device_id=device, device_id_type=MESH)
+
+    @pl.when(first_member)
+    def _():
+        signal(barrier, near)
+
+    signal(barrier, ring_peers)
 
     load_x = pltpu.make_async_copy(tokens_in, tokens, load_sem.at[3])
     load_dy = pltpu.make_async_copy(cotangent_in, cotangent, load_sem.at[4])
@@ -273,7 +284,16 @@
 
     load_x.wait()
     pack_rest(send.at[0], lax.fori_loop(0, J, gather_x, zero_rest))
-    pl.semaphore_wait(barrier, len(peers))
+
+    @pl.when(jnp.logical_not(first_member))
+    def _():
+        pl.semaphore_wait(barrier, len(ring_peers))
+
+    @pl.when(first_member)
+    def _():
+        pl.semaphore_wait(barrier, len(ring_peers) + len(near))
+        signal(ring_sem, near)
+
     ex_x.begin()
     scaled_masks()
     load_dy.wait()
@@ -286,7 +306,18 @@
     ]
     for store in stores:
         store.start()
+
+    @pl.when(first_member)
+    def _():
+        pl.semaphore_wait(ring_sem, len(near))
+        signal(near_sem, ring_peers)
+
     ex_x.arrived()
+
+    @pl.when(jnp.logical_not(first_member))
+    def _():
+        pl.semaphore_wait(near_sem, 1)
+
     swap_x = remote(xr.at[0], xr.at[1], 28, partner)
     start([swap_x])
     for load in loads:
@@ -581,6 +612,8 @@
             pltpu.SemaphoreType.DMA((4,)),
             pltpu.SemaphoreType.DMA((56,)),
             pltpu.SemaphoreType.DMA((56,)),
+            pltpu.SemaphoreType.REGULAR,
+            pltpu.SemaphoreType.REGULAR,
         ],
         compiler_params=pltpu.CompilerParams(
             collective_id=0, has_side_effects=True, vmem_limit_bytes=63_000_000

time: 123 us -> 123 us (level)
  no operation moved by 1% of the time
where the time goes in v3:
time: 123 us
  Pallas kernels  122 us (99%)
    pallas_call x1, Pallas kernels, per_device(): pl.pallas_call(kernel, out_shape=outs[0:1] + masks + outs[1:], in_specs=[...  119 us
    pallas_call x1, Pallas kernels, per_device(): pl.pallas_call(finish, out_shape=outs[0:1] + outs, in_specs=[hbm] * 7, ou...  3.25 us

profile of v3, /device:TPU:1, one launch (start us, length us, event | category | flops | bytes accessed | tf_op | source)
XLA Modules:
  0.0 122.7 jit_solution(4742934103980125287)
XLA Ops:
  0.6 118.8 %moe.1 = (bf16[128,2048]{1,0:T(8,128)(2,1)}, bf16[8,144,512]{2,1,0:T(8,128)(2,1)}, bf16[128,256]{1,0:T(8,128)(2,1)}, bf16[4,128,128]{2,1,0:T(8,128)(2,1)}, f32[1...) custom-call(s32[2,128]{1,0:T(2,128)} %bitcast.2, s32[2,128]{1,0:T(2,128)} %bitcast.3, ...), custom_call_target="tpu_custom_call" | custom-call | tf_op jit(solution)/shard_map/moe/pallas_call | solution.py:574
  119.5 3.2 %finish.1 = (bf16[128,2048]{1,0:T(8,128)(2,1)}, bf16[128,2048]{1,0:T(8,128)(2,1)}, f32[128,512]{1,0:T(8,128)}, f32[128,512]{1,0:T(8,128)}, f32[512,128]{1,0:T(8,128)}) custom-call(bf16[8,144,512]{2,1,0:T(8,128)(2,1)} %get-tuple-element.17.dx_in, bf16[128,256]{1,0:T(8,128)(2,1)} %get-tuple-element.18.left_in, ...), custom_call_target="tpu_custom_call" | custom-call | tf_op jit(solution)/shard_map/finish/pallas_call | solution.py:623

commit v4 on v3

--- a/solution.py
+++ b/solution.py
@@ -430,11 +430,11 @@
         ring.begin()
 
     swap = partials(1, lambda j: dot_cols(bg[...], wgu[cols(j), :]))
-    for ring in ring_a:
-        ring.relay()
     swap.wait_recv()
     add_partials(1, 3)
     ex_dx.begin()
+    for ring in ring_a:
+        ring.relay()
 
     def combine(j, carry):
         rows = back[:, main_rows(j), :].reshape(E * MAIN, W)

time: 123 us -> 122 us (level)
  Pallas kernels: 122 us -> 120 us
    pallas_call x1, Pallas kernels: 119 us -> 117 us  [per_device(): pl.pallas_call(kernel, out_shape=outs[0:1] + masks + outs[1:], in_specs=[...]
where the time goes in v4:
time: 122 us; the launch traced here: 121 us
  Pallas kernels  120 us (98%)
    pallas_call x1, Pallas kernels, per_device(): pl.pallas_call(kernel, out_shape=outs[0:1] + masks + outs[1:], in_specs=[...  117 us
    pallas_call x1, Pallas kernels, per_device(): pl.pallas_call(finish, out_shape=outs[0:1] + outs, in_specs=[hbm] * 7, ou...  3.25 us

profile of v4, /device:TPU:1, one launch (start us, length us, event | category | flops | bytes accessed | tf_op | source)
XLA Modules:
  0.0 120.7 jit_solution(1297662353488676457)
XLA Ops:
  0.6 116.8 %moe.1 = (bf16[128,2048]{1,0:T(8,128)(2,1)}, bf16[8,144,512]{2,1,0:T(8,128)(2,1)}, bf16[128,256]{1,0:T(8,128)(2,1)}, bf16[4,128,128]{2,1,0:T(8,128)(2,1)}, f32[1...) custom-call(s32[2,128]{1,0:T(2,128)} %bitcast.2, s32[2,128]{1,0:T(2,128)} %bitcast.3, ...), custom_call_target="tpu_custom_call" | custom-call | tf_op jit(solution)/shard_map/moe/pallas_call | solution.py:574
  117.5 3.2 %finish.1 = (bf16[128,2048]{1,0:T(8,128)(2,1)}, bf16[128,2048]{1,0:T(8,128)(2,1)}, f32[128,512]{1,0:T(8,128)}, f32[128,512]{1,0:T(8,128)}, f32[512,128]{1,0:T(8,128)}) custom-call(bf16[8,144,512]{2,1,0:T(8,128)(2,1)} %get-tuple-element.17.dx_in, bf16[128,256]{1,0:T(8,128)(2,1)} %get-tuple-element.18.left_in, ...), custom_call_target="tpu_custom_call" | custom-call | tf_op jit(solution)/shard_map/finish/pallas_call | solution.py:623
